TPU v7x, 128 devices: a whole 4x4x4 slice. The times are simulated.
128 devices in a mesh: shot: 4 (over y_lo, core), gx: 4 (over z), gy: 8 (over x, y_hi).
Axes of the slice: x: 4, y: 4 (y_hi: 2, y_lo: 2; y = y_hi * 2 + y_lo), z: 4, core: 2. Of those that a mesh axis runs over, the one named last changes fastest.
Arguments:
- model_tiles: float32 [256, 256, 128], P(('shot', 'gx'), 'gy'), may hold values from 0.2 to 0.45
- owner_map: int32 [16], replicated, may hold values from 0 to 15, each once
- offsets: int32 [4], P('shot'), may hold values from 0 to 12
- field_now: float32 [4, 2, 64, 256, 128], P('shot', None, 'gx', 'gy'), may hold values from -6 to 6
- field_prev: float32 [4, 2, 64, 256, 128], P('shot', None, 'gx', 'gy'), may hold values from -6 to 6
- sources: int32 [4, 2, 3], P('shot'), may hold values from 0 to 255, as said below
- wavelet: float32 [4, 2, 8], P('shot'), may hold values from -6 to 6
- receivers: int32 [4, 256, 3], P('shot'), may hold values from 0 to 255, as said below
Outputs:
- out_now: float32 [4, 2, 64, 256, 128], P('shot', None, 'gx', 'gy')
- out_prev: float32 [4, 2, 64, 256, 128], P('shot', None, 'gx', 'gy')
- traces: float32 [4, 2, 256, 8], P('shot')
Inputs may be any that keep to these rules, and one draw needn't show every extreme that they name: `sources`: each row is a cell of the group's aperture: first entry below 64, second below 256, third below 128. `receivers`: each row is a cell of the group's aperture: first entry below 64, second below 256, third below 128.
All inputs are finite; a program needn't handle non-finite values.
Results may differ from a plain program's by a relative error of at most 0.0003.
Values sent between devices are 32-bit elements; how exact they have to be, the bound alone decides.
A program may use at most 128 MiB of HBM per device.

v0:
```python
import jax
import jax.numpy as jnp
from jax import lax
from jax.sharding import PartitionSpec as P

STEPS = 8
center_weight = -2.5
near_weight = 4.0 / 3.0
far_weight = -1.0 / 12.0
damp_peak = 0.3


def extended_2(cells, sides, width):
    for axis, dim in sides:
        count = lax.axis_size(axis)
        ends = count - 1
        head = lax.slice_in_dim(cells, 0, width, axis=dim)
        tail = lax.slice_in_dim(cells, cells.shape[dim] - width, cells.shape[dim], axis=dim)
        cells = jnp.concatenate(
            [
                lax.ppermute(tail, axis, [(i, (i + 1) % count) for i in range(ends)]),
                cells,
                lax.ppermute(head, axis, [((i + 1) % count, i) for i in range(ends)]),
            ],
            axis=dim,
        )
    return cells


def depth_ahead(field, reach):
    filler = jnp.zeros(field.shape[:-1] + (reach,), field.dtype)
    return jnp.concatenate([field[..., reach:], filler], axis=-1)


def depth_behind(field, reach):
    filler = jnp.zeros(field.shape[:-1] + (reach,), field.dtype)
    return jnp.concatenate([filler, field[..., :-reach]], axis=-1)


def laplace(extended):
    middle = extended[:, 2:-2, 2:-2]
    along_x = (
        center_weight * middle
        + near_weight * (extended[:, 3:-1, 2:-2] + extended[:, 1:-3, 2:-2])
        + far_weight * (extended[:, 4:, 2:-2] + extended[:, :-4, 2:-2])
    )
    along_y = (
        center_weight * middle
        + near_weight * (extended[:, 2:-2, 3:-1] + extended[:, 2:-2, 1:-3])
        + far_weight * (extended[:, 2:-2, 4:] + extended[:, 2:-2, :-4])
    )
    along_z = (
        center_weight * middle
        + near_weight * (depth_ahead(middle, 1) + depth_behind(middle, 1))
        + far_weight * (depth_ahead(middle, 2) + depth_behind(middle, 2))
    )
    return along_x + along_y + along_z


def damping(x_cells, y_cells, width, x_total, y_total):
    x_depth = (
        jnp.maximum(width - jnp.minimum(x_cells + 1, x_total - x_cells), 0).astype(jnp.float32)
        / width
    )
    y_depth = (
        jnp.maximum(width - jnp.minimum(y_cells + 1, y_total - y_cells), 0).astype(jnp.float32)
        / width
    )
    return damp_peak * (x_depth[:, None] * x_depth[:, None] + y_depth[None, :] * y_depth[None, :])


def injection(x_cells, y_cells, z_cells, source_cells, amplitude):
    on_x = (x_cells[None, :] == source_cells[:, 0:1]).astype(jnp.float32)
    on_y = (y_cells[None, :] == source_cells[:, 1:2]).astype(jnp.float32)
    on_z = (z_cells[None, :] == source_cells[:, 2:3]).astype(jnp.float32)
    return (
        amplitude[:, None, None, None]
        * on_x[:, :, None, None]
        * on_y[:, None, :, None]
        * on_z[:, None, None, :]
    )


def advance(extended, previous, coef, damp, inject):
    middle = extended[:, 2:-2, 2:-2]
    return (2.0 * middle - (1.0 - damp) * previous + coef * laplace(extended) + inject) / (
        1.0 + damp
    )


def sample(field, receiver_cells, x_start, y_start):
    size_x, size_y = (field.shape[1], field.shape[2])
    local_x = receiver_cells[:, 0] - x_start
    local_y = receiver_cells[:, 1] - y_start
    inside = (local_x >= 0) & (local_x < size_x) & (local_y >= 0) & (local_y < size_y)
    values = field[
        :, jnp.clip(local_x, 0, size_x - 1), jnp.clip(local_y, 0, size_y - 1), receiver_cells[:, 2]
    ]
    return jnp.where(inside[None, :], values, 0.0)


def local(model_tiles, owner_map, offsets, field_now, field_prev, sources, wavelet, receivers):
    block_x, block_y, depth = model_tiles.shape
    column_index = lax.axis_index("gx")
    row_index = lax.axis_index("gy")
    across = lax.axis_size("gx")
    total_x = block_x * across
    total_y = block_y * lax.axis_size("gy")
    shift_x = offsets[0]
    tile_total = owner_map.shape[0]
    column_ids = jnp.arange(tile_total, dtype=jnp.int32)
    wanted = jnp.sum(jnp.where(column_ids == shift_x + column_index, owner_map, 0))
    piece = lax.all_gather(model_tiles, ("shot", "gx"), axis=0, tiled=True)
    rows = wanted * block_x + jnp.arange(block_x, dtype=jnp.int32)
    inside = (rows >= 0) & (rows < piece.shape[0])
    taken = jnp.take(piece, jnp.clip(rows, 0, piece.shape[0] - 1), axis=0)
    speed = jnp.where(inside[:, None, None], taken, jnp.zeros_like(model_tiles))
    coef = speed * speed
    current = field_now[0]
    previous = field_prev[0]
    source_cells = sources[0]
    amplitudes = wavelet[0]
    receiver_cells = receivers[0]
    x_start = column_index * block_x
    y_start = row_index * block_y
    x_here = x_start + jnp.arange(block_x, dtype=jnp.int32)
    y_here = y_start + jnp.arange(block_y, dtype=jnp.int32)
    z_cells = jnp.arange(depth, dtype=jnp.int32)
    damp = damping(x_here, y_here, block_x, total_x, total_y)[:, :, None]
    recorded = []
    for step in range(STEPS):
        extended = extended_2(current, (("gx", 1), ("gy", 2)), 2)
        inject = injection(x_here, y_here, z_cells, source_cells, amplitudes[:, step])
        fresh = advance(extended, previous, coef, damp, inject)
        recorded.append(sample(fresh, receiver_cells, x_start, y_start))
        previous = current
        current = fresh
    traces = lax.psum(jnp.stack(recorded, axis=-1), ("gx", "gy"))
    return (current[None], previous[None], traces[None])


def solution(mesh):
    return jax.shard_map(
        local,
        mesh=mesh,
        in_specs=(
            P(("shot", "gx"), "gy", None),
            P(),
            P("shot"),
            P("shot", None, "gx", "gy", None),
            P("shot", None, "gx", "gy", None),
            P("shot", None, None),
            P("shot", None, None),
            P("shot", None, None),
        ),
        out_specs=(
            P("shot", None, "gx", "gy", None),
            P("shot", None, "gx", "gy", None),
            P("shot", None, None, None),
        ),
        check_vma=False,
    )
```

profile of v0, /device:TPU:0, one launch (start us, length us, event | category | flops | bytes accessed | tf_op | source)
XLA Modules:
  0.0 552.9 jit_solution(16876477504030605119)
XLA Ops:
  28.2 6.1 %collective-permute-start.3 = (f32[2,20,2,128]{3,2,1,0:T(2,128)S(1)}, f32[2,20,2,128]{3,2,1,0:T(2,128)S(1)}, u32[]{:S(2)}, u32[]{:S(2)}) collective-permute-start(f32[2,20,2,128]{3,2,1,0:T(2,128)S(1)} %get-tuple-element.57), channel_id=1, source_target_pairs={{0,1},{1,2},{2,3},{3,4},{4,5},{5,6},{6,7},{8,9},{9,10},{10,11},{11... | collective-permute-start | bytes 122888 | tf_op jit(solution)/shard_map/ppermute | solution.py:21
  37.5 24.6 %all-gather.2.cloned.1.call-done = f32[256,32,128]{2,1,0:T(8,128)} async-done(((f32[16,32,128]{2,1,0:T(8,128)}), f32[256,32,128]{2,1,0:T(8,128)}) %all-gather.2.cloned.1.call-update) | async-done | bytes 4194320 | tf_op jit(solution)/shard_map/all_gather | solution.py:113
  77.4 6.1 %collective-permute-start.7 = (f32[2,20,2,128]{3,2,1,0:T(2,128)S(1)}, f32[2,20,2,128]{3,2,1,0:T(2,128)S(1)}, u32[]{:S(2)}, u32[]{:S(2)}) collective-permute-start(f32[2,20,2,128]{3,2,1,0:T(2,128)S(1)} %get-tuple-element.53), channel_id=1, source_target_pairs={{0,1},{1,2},{2,3},{3,4},{4,5},{5,6},{6,7},{8,9},{9,10},{10,11},{11... | collective-permute-start | bytes 122888 | tf_op jit(solution)/shard_map/ppermute | solution.py:21
  84.4 16.7 %copy.515 = f32[2,16,32,128]{0,3,2,1:T(8,128)} copy(f32[2,16,32,128]{3,2,1,0:T(8,128)S(1)} %fusion.94) | data formatting | bytes 1048576 | tf_op jit(solution)/shard_map/div | solution.py:86
  107.5 5.0 collective-permute-start.9
  115.8 6.5 %collective-permute-start.11 = (f32[2,20,2,128]{3,2,1,0:T(2,128)S(1)}, f32[2,20,2,128]{3,2,1,0:T(2,128)S(1)}, u32[]{:S(2)}, u32[]{:S(2)}) collective-permute-start(f32[2,20,2,128]{3,2,1,0:T(2,128)S(1)} %get-tuple-element.49), channel_id=1, source_target_pairs={{0,1},{1,2},{2,3},{3,4},{4,5},{5,6},{6,7},{8,9},{9,10},{10,11},{11... | collective-permute-start | bytes 122888 | tf_op jit(solution)/shard_map/ppermute | solution.py:21
  123.2 16.7 %copy.516 = f32[2,16,32,128]{0,3,2,1:T(8,128)} copy(f32[2,16,32,128]{3,2,1,0:T(8,128)S(1)} %fusion.82) | data formatting | bytes 1048576 | tf_op jit(solution)/shard_map/div | solution.py:86
  146.4 4.9 collective-permute-start.13
  154.5 6.9 %collective-permute-start.15 = (f32[2,20,2,128]{3,2,1,0:T(2,128)S(1)}, f32[2,20,2,128]{3,2,1,0:T(2,128)S(1)}, u32[]{:S(2)}, u32[]{:S(2)}) collective-permute-start(f32[2,20,2,128]{3,2,1,0:T(2,128)S(1)} %get-tuple-element.45), channel_id=1, source_target_pairs={{0,1},{1,2},{2,3},{3,4},{4,5},{5,6},{6,7},{8,9},{9,10},{10,11},{11... | collective-permute-start | bytes 122888 | tf_op jit(solution)/shard_map/ppermute | solution.py:21
  162.4 16.7 %copy.517 = f32[2,16,32,128]{0,3,2,1:T(8,128)} copy(f32[2,16,32,128]{3,2,1,0:T(8,128)S(1)} %fusion.70) | data formatting | bytes 1048576 | tf_op jit(solution)/shard_map/div | solution.py:86
  185.6 4.9 collective-permute-start.17
  193.7 7.1 %collective-permute-start.19 = (f32[2,20,2,128]{3,2,1,0:T(2,128)S(1)}, f32[2,20,2,128]{3,2,1,0:T(2,128)S(1)}, u32[]{:S(2)}, u32[]{:S(2)}) collective-permute-start(f32[2,20,2,128]{3,2,1,0:T(2,128)S(1)} %get-tuple-element.41), channel_id=1, source_target_pairs={{0,1},{1,2},{2,3},{3,4},{4,5},{5,6},{6,7},{8,9},{9,10},{10,11},{11... | collective-permute-start | bytes 122888 | tf_op jit(solution)/shard_map/ppermute | solution.py:21
  201.7 16.7 %copy.518 = f32[2,16,32,128]{0,3,2,1:T(8,128)} copy(f32[2,16,32,128]{3,2,1,0:T(8,128)S(1)} %fusion.58) | data formatting | bytes 1048576 | tf_op jit(solution)/shard_map/div | solution.py:86
  224.9 4.9 collective-permute-start.21
  233.0 6.9 %collective-permute-start.23 = (f32[2,20,2,128]{3,2,1,0:T(2,128)S(1)}, f32[2,20,2,128]{3,2,1,0:T(2,128)S(1)}, u32[]{:S(2)}, u32[]{:S(2)}) collective-permute-start(f32[2,20,2,128]{3,2,1,0:T(2,128)S(1)} %get-tuple-element.37), channel_id=1, source_target_pairs={{0,1},{1,2},{2,3},{3,4},{4,5},{5,6},{6,7},{8,9},{9,10},{10,11},{11... | collective-permute-start | bytes 122888 | tf_op jit(solution)/shard_map/ppermute | solution.py:21
  240.9 16.7 %copy.519 = f32[2,16,32,128]{0,3,2,1:T(8,128)} copy(f32[2,16,32,128]{3,2,1,0:T(8,128)S(1)} %fusion.46) | data formatting | bytes 1048576 | tf_op jit(solution)/shard_map/div | solution.py:86
  264.1 4.9 collective-permute-start.25
  272.2 6.9 %collective-permute-start.27 = (f32[2,20,2,128]{3,2,1,0:T(2,128)S(1)}, f32[2,20,2,128]{3,2,1,0:T(2,128)S(1)}, u32[]{:S(2)}, u32[]{:S(2)}) collective-permute-start(f32[2,20,2,128]{3,2,1,0:T(2,128)S(1)} %get-tuple-element.33), channel_id=1, source_target_pairs={{0,1},{1,2},{2,3},{3,4},{4,5},{5,6},{6,7},{8,9},{9,10},{10,11},{11... | collective-permute-start | bytes 122888 | tf_op jit(solution)/shard_map/ppermute | solution.py:21
  280.1 16.7 %copy.520 = f32[2,16,32,128]{0,3,2,1:T(8,128)} copy(f32[2,16,32,128]{3,2,1,0:T(8,128)S(1)} %fusion.34) | data formatting | bytes 1048576 | tf_op jit(solution)/shard_map/div | solution.py:86
  303.2 4.9 collective-permute-start.29
  311.3 7.2 %collective-permute-start.31 = (f32[2,20,2,128]{3,2,1,0:T(2,128)S(1)}, f32[2,20,2,128]{3,2,1,0:T(2,128)S(1)}, u32[]{:S(2)}, u32[]{:S(2)}) collective-permute-start(f32[2,20,2,128]{3,2,1,0:T(2,128)S(1)} %get-tuple-element.29), channel_id=1, source_target_pairs={{0,1},{1,2},{2,3},{3,4},{4,5},{5,6},{6,7},{8,9},{9,10},{10,11},{11... | collective-permute-start | bytes 122888 | tf_op jit(solution)/shard_map/ppermute | solution.py:21
  319.5 16.7 %copy.521 = f32[2,16,32,128]{0,3,2,1:T(8,128)} copy(f32[2,16,32,128]{3,2,1,0:T(8,128)S(1)} %fusion.22) | data formatting | bytes 1048576 | tf_op jit(solution)/shard_map/div | solution.py:86
  341.3 16.8 %copy.522 = f32[2,16,32,128]{0,3,2,1:T(8,128)} copy(f32[2,16,32,128]{3,2,1,0:T(8,128)S(1)} %fusion.10) | data formatting | bytes 1048576 | tf_op jit(solution)/shard_map/div | solution.py:86
  362.6 183.4 %psum.7 = f32[1,2,256,8]{2,3,1,0:T(8,128)} all-reduce(f32[1,2,256,8]{2,3,1,0:T(8,128)S(1)} %bitcast.70), channel_id=1, replica_groups=mesh['shot'=4,'gx'=4,'gy'=8] {'gx','gy'}, use_global_device_ids=true, to_apply=%region_1.2 | all-reduce | flops 4096 | bytes 32768 | tf_op jit(solution)/shard_map/psum | solution.py:138
  (164 shorter events, 112.2 us)
Async XLA Ops:
  7.2 54.9 %all-gather.2.cloned.1.call-start = ((), (), s32[]{:S(2)}) async-start(), calls=%async_computation | async-start | bytes 4456448 | tf_op jit(solution)/shard_map/all_gather | solution.py:113
  8.8 17.0 %collective-permute-start = (f32[2,2,32,128]{3,2,1,0:T(8,128)S(1)}, f32[2,2,32,128]{3,2,1,0:T(8,128)S(1)}, u32[]{:S(2)}, u32[]{:S(2)}) collective-permute-start(f32[2,2,32,128]{3,2,1,0:T(8,128)S(1)} %get-tuple-element.104), channel_id=1, source_target_pairs={{8,0},{16,8},{24,16},{9,1},{17,9},{25,17},{10,2},{18,10},{26,18},{... | collective-permute-start | bytes 196616 | tf_op jit(solution)/shard_map/ppermute | solution.py:23
  10.1 15.8 %collective-permute-start.1 = (f32[2,2,32,128]{3,2,1,0:T(8,128)S(1)}, f32[2,2,32,128]{3,2,1,0:T(8,128)S(1)}, u32[]{:S(2)}, u32[]{:S(2)}) collective-permute-start(f32[2,2,32,128]{3,2,1,0:T(8,128)S(1)} %get-tuple-element.105), channel_id=1, source_target_pairs={{0,8},{8,16},{16,24},{1,9},{9,17},{17,25},{2,10},{10,18},{18,26},{... | collective-permute-start | bytes 196616 | tf_op jit(solution)/shard_map/ppermute | solution.py:21
  26.9 7.7 %collective-permute-start.2 = (f32[2,20,2,128]{3,2,1,0:T(2,128)S(1)}, f32[2,20,2,128]{3,2,1,0:T(2,128)S(1)}, u32[]{:S(2)}, u32[]{:S(2)}) collective-permute-start(f32[2,20,2,128]{3,2,1,0:T(2,128)S(1)} %get-tuple-element.56), channel_id=1, source_target_pairs={{1,0},{2,1},{3,2},{4,3},{5,4},{6,5},{7,6},{9,8},{10,9},{11,10},{12... | collective-permute-start | bytes 122888 | tf_op jit(solution)/shard_map/ppermute | solution.py:23
  28.2 7.9 %collective-permute-start.3 = (f32[2,20,2,128]{3,2,1,0:T(2,128)S(1)}, f32[2,20,2,128]{3,2,1,0:T(2,128)S(1)}, u32[]{:S(2)}, u32[]{:S(2)}) collective-permute-start(f32[2,20,2,128]{3,2,1,0:T(2,128)S(1)} %get-tuple-element.57), channel_id=1, source_target_pairs={{0,1},{1,2},{2,3},{3,4},{4,5},{5,6},{6,7},{8,9},{9,10},{10,11},{11... | collective-permute-start | bytes 122888 | tf_op jit(solution)/shard_map/ppermute | solution.py:21
  68.1 6.8 %collective-permute-start.4 = (f32[2,2,32,128]{3,2,1,0:T(8,128)S(1)}, f32[2,2,32,128]{3,2,1,0:T(8,128)S(1)}, u32[]{:S(2)}, u32[]{:S(2)}) collective-permute-start(f32[2,2,32,128]{3,2,1,0:T(8,128)S(1)} %get-tuple-element.98), channel_id=1, source_target_pairs={{8,0},{16,8},{24,16},{9,1},{17,9},{25,17},{10,2},{18,10},{26,18},{... | collective-permute-start | bytes 196616 | tf_op jit(solution)/shard_map/ppermute | solution.py:23
  76.1 28.0 %collective-permute-start.6 = (f32[2,20,2,128]{3,2,1,0:T(2,128)S(1)}, f32[2,20,2,128]{3,2,1,0:T(2,128)S(1)}, u32[]{:S(2)}, u32[]{:S(2)}) collective-permute-start(f32[2,20,2,128]{3,2,1,0:T(2,128)S(1)} %get-tuple-element.52), channel_id=1, source_target_pairs={{1,0},{2,1},{3,2},{4,3},{5,4},{6,5},{7,6},{9,8},{10,9},{11,10},{12... | collective-permute-start | bytes 122888 | tf_op jit(solution)/shard_map/ppermute | solution.py:23
  77.4 26.7 %collective-permute-start.7 = (f32[2,20,2,128]{3,2,1,0:T(2,128)S(1)}, f32[2,20,2,128]{3,2,1,0:T(2,128)S(1)}, u32[]{:S(2)}, u32[]{:S(2)}) collective-permute-start(f32[2,20,2,128]{3,2,1,0:T(2,128)S(1)} %get-tuple-element.53), channel_id=1, source_target_pairs={{0,1},{1,2},{2,3},{3,4},{4,5},{5,6},{6,7},{8,9},{9,10},{10,11},{11... | collective-permute-start | bytes 122888 | tf_op jit(solution)/shard_map/ppermute | solution.py:21
  107.5 6.9 %collective-permute-start.9 = (f32[2,2,32,128]{3,2,1,0:T(8,128)S(1)}, f32[2,2,32,128]{3,2,1,0:T(8,128)S(1)}, u32[]{:S(2)}, u32[]{:S(2)}) collective-permute-start(f32[2,2,32,128]{3,2,1,0:T(8,128)S(1)} %get-tuple-element.93), channel_id=1, source_target_pairs={{0,8},{8,16},{16,24},{1,9},{9,17},{17,25},{2,10},{10,18},{18,26},{... | collective-permute-start | bytes 196616 | tf_op jit(solution)/shard_map/ppermute | solution.py:21
  114.5 28.5 %collective-permute-start.10 = (f32[2,20,2,128]{3,2,1,0:T(2,128)S(1)}, f32[2,20,2,128]{3,2,1,0:T(2,128)S(1)}, u32[]{:S(2)}, u32[]{:S(2)}) collective-permute-start(f32[2,20,2,128]{3,2,1,0:T(2,128)S(1)} %get-tuple-element.48), channel_id=1, source_target_pairs={{1,0},{2,1},{3,2},{4,3},{5,4},{6,5},{7,6},{9,8},{10,9},{11,10},{12... | collective-permute-start | bytes 122888 | tf_op jit(solution)/shard_map/ppermute | solution.py:23
  115.8 27.2 %collective-permute-start.11 = (f32[2,20,2,128]{3,2,1,0:T(2,128)S(1)}, f32[2,20,2,128]{3,2,1,0:T(2,128)S(1)}, u32[]{:S(2)}, u32[]{:S(2)}) collective-permute-start(f32[2,20,2,128]{3,2,1,0:T(2,128)S(1)} %get-tuple-element.49), channel_id=1, source_target_pairs={{0,1},{1,2},{2,3},{3,4},{4,5},{5,6},{6,7},{8,9},{9,10},{10,11},{11... | collective-permute-start | bytes 122888 | tf_op jit(solution)/shard_map/ppermute | solution.py:21
  146.4 6.8 %collective-permute-start.13 = (f32[2,2,32,128]{3,2,1,0:T(8,128)S(1)}, f32[2,2,32,128]{3,2,1,0:T(8,128)S(1)}, u32[]{:S(2)}, u32[]{:S(2)}) collective-permute-start(f32[2,2,32,128]{3,2,1,0:T(8,128)S(1)} %get-tuple-element.87), channel_id=1, source_target_pairs={{0,8},{8,16},{16,24},{1,9},{9,17},{17,25},{2,10},{10,18},{18,26},{... | collective-permute-start | bytes 196616 | tf_op jit(solution)/shard_map/ppermute | solution.py:21
  153.2 28.9 %collective-permute-start.14 = (f32[2,20,2,128]{3,2,1,0:T(2,128)S(1)}, f32[2,20,2,128]{3,2,1,0:T(2,128)S(1)}, u32[]{:S(2)}, u32[]{:S(2)}) collective-permute-start(f32[2,20,2,128]{3,2,1,0:T(2,128)S(1)} %get-tuple-element.44), channel_id=1, source_target_pairs={{1,0},{2,1},{3,2},{4,3},{5,4},{6,5},{7,6},{9,8},{10,9},{11,10},{12... | collective-permute-start | bytes 122888 | tf_op jit(solution)/shard_map/ppermute | solution.py:23
  154.5 27.6 %collective-permute-start.15 = (f32[2,20,2,128]{3,2,1,0:T(2,128)S(1)}, f32[2,20,2,128]{3,2,1,0:T(2,128)S(1)}, u32[]{:S(2)}, u32[]{:S(2)}) collective-permute-start(f32[2,20,2,128]{3,2,1,0:T(2,128)S(1)} %get-tuple-element.45), channel_id=1, source_target_pairs={{0,1},{1,2},{2,3},{3,4},{4,5},{5,6},{6,7},{8,9},{9,10},{10,11},{11... | collective-permute-start | bytes 122888 | tf_op jit(solution)/shard_map/ppermute | solution.py:21
  185.6 6.8 %collective-permute-start.17 = (f32[2,2,32,128]{3,2,1,0:T(8,128)S(1)}, f32[2,2,32,128]{3,2,1,0:T(8,128)S(1)}, u32[]{:S(2)}, u32[]{:S(2)}) collective-permute-start(f32[2,2,32,128]{3,2,1,0:T(8,128)S(1)} %get-tuple-element.81), channel_id=1, source_target_pairs={{0,8},{8,16},{16,24},{1,9},{9,17},{17,25},{2,10},{10,18},{18,26},{... | collective-permute-start | bytes 196616 | tf_op jit(solution)/shard_map/ppermute | solution.py:21
  192.4 29.1 %collective-permute-start.18 = (f32[2,20,2,128]{3,2,1,0:T(2,128)S(1)}, f32[2,20,2,128]{3,2,1,0:T(2,128)S(1)}, u32[]{:S(2)}, u32[]{:S(2)}) collective-permute-start(f32[2,20,2,128]{3,2,1,0:T(2,128)S(1)} %get-tuple-element.40), channel_id=1, source_target_pairs={{1,0},{2,1},{3,2},{4,3},{5,4},{6,5},{7,6},{9,8},{10,9},{11,10},{12... | collective-permute-start | bytes 122888 | tf_op jit(solution)/shard_map/ppermute | solution.py:23
  193.7 27.8 %collective-permute-start.19 = (f32[2,20,2,128]{3,2,1,0:T(2,128)S(1)}, f32[2,20,2,128]{3,2,1,0:T(2,128)S(1)}, u32[]{:S(2)}, u32[]{:S(2)}) collective-permute-start(f32[2,20,2,128]{3,2,1,0:T(2,128)S(1)} %get-tuple-element.41), channel_id=1, source_target_pairs={{0,1},{1,2},{2,3},{3,4},{4,5},{5,6},{6,7},{8,9},{9,10},{10,11},{11... | collective-permute-start | bytes 122888 | tf_op jit(solution)/shard_map/ppermute | solution.py:21
  231.7 28.9 %collective-permute-start.22 = (f32[2,20,2,128]{3,2,1,0:T(2,128)S(1)}, f32[2,20,2,128]{3,2,1,0:T(2,128)S(1)}, u32[]{:S(2)}, u32[]{:S(2)}) collective-permute-start(f32[2,20,2,128]{3,2,1,0:T(2,128)S(1)} %get-tuple-element.36), channel_id=1, source_target_pairs={{1,0},{2,1},{3,2},{4,3},{5,4},{6,5},{7,6},{9,8},{10,9},{11,10},{12... | collective-permute-start | bytes 122888 | tf_op jit(solution)/shard_map/ppermute | solution.py:23
  233.0 27.6 %collective-permute-start.23 = (f32[2,20,2,128]{3,2,1,0:T(2,128)S(1)}, f32[2,20,2,128]{3,2,1,0:T(2,128)S(1)}, u32[]{:S(2)}, u32[]{:S(2)}) collective-permute-start(f32[2,20,2,128]{3,2,1,0:T(2,128)S(1)} %get-tuple-element.37), channel_id=1, source_target_pairs={{0,1},{1,2},{2,3},{3,4},{4,5},{5,6},{6,7},{8,9},{9,10},{10,11},{11... | collective-permute-start | bytes 122888 | tf_op jit(solution)/shard_map/ppermute | solution.py:21
  264.1 6.8 %collective-permute-start.25 = (f32[2,2,32,128]{3,2,1,0:T(8,128)S(1)}, f32[2,2,32,128]{3,2,1,0:T(8,128)S(1)}, u32[]{:S(2)}, u32[]{:S(2)}) collective-permute-start(f32[2,2,32,128]{3,2,1,0:T(8,128)S(1)} %get-tuple-element.69), channel_id=1, source_target_pairs={{0,8},{8,16},{16,24},{1,9},{9,17},{17,25},{2,10},{10,18},{18,26},{... | collective-permute-start | bytes 196616 | tf_op jit(solution)/shard_map/ppermute | solution.py:21
  270.9 28.9 %collective-permute-start.26 = (f32[2,20,2,128]{3,2,1,0:T(2,128)S(1)}, f32[2,20,2,128]{3,2,1,0:T(2,128)S(1)}, u32[]{:S(2)}, u32[]{:S(2)}) collective-permute-start(f32[2,20,2,128]{3,2,1,0:T(2,128)S(1)} %get-tuple-element.32), channel_id=1, source_target_pairs={{1,0},{2,1},{3,2},{4,3},{5,4},{6,5},{7,6},{9,8},{10,9},{11,10},{12... | collective-permute-start | bytes 122888 | tf_op jit(solution)/shard_map/ppermute | solution.py:23
  272.2 27.6 %collective-permute-start.27 = (f32[2,20,2,128]{3,2,1,0:T(2,128)S(1)}, f32[2,20,2,128]{3,2,1,0:T(2,128)S(1)}, u32[]{:S(2)}, u32[]{:S(2)}) collective-permute-start(f32[2,20,2,128]{3,2,1,0:T(2,128)S(1)} %get-tuple-element.33), channel_id=1, source_target_pairs={{0,1},{1,2},{2,3},{3,4},{4,5},{5,6},{6,7},{8,9},{9,10},{10,11},{11... | collective-permute-start | bytes 122888 | tf_op jit(solution)/shard_map/ppermute | solution.py:21
  310.0 29.1 %collective-permute-start.30 = (f32[2,20,2,128]{3,2,1,0:T(2,128)S(1)}, f32[2,20,2,128]{3,2,1,0:T(2,128)S(1)}, u32[]{:S(2)}, u32[]{:S(2)}) collective-permute-start(f32[2,20,2,128]{3,2,1,0:T(2,128)S(1)} %get-tuple-element.28), channel_id=1, source_target_pairs={{1,0},{2,1},{3,2},{4,3},{5,4},{6,5},{7,6},{9,8},{10,9},{11,10},{12... | collective-permute-start | bytes 122888 | tf_op jit(solution)/shard_map/ppermute | solution.py:23
  311.3 27.8 %collective-permute-start.31 = (f32[2,20,2,128]{3,2,1,0:T(2,128)S(1)}, f32[2,20,2,128]{3,2,1,0:T(2,128)S(1)}, u32[]{:S(2)}, u32[]{:S(2)}) collective-permute-start(f32[2,20,2,128]{3,2,1,0:T(2,128)S(1)} %get-tuple-element.29), channel_id=1, source_target_pairs={{0,1},{1,2},{2,3},{3,4},{4,5},{5,6},{6,7},{8,9},{9,10},{10,11},{11... | collective-permute-start | bytes 122888 | tf_op jit(solution)/shard_map/ppermute | solution.py:21
  (22 other events, 717.0 us)
Sparse Core Ops, SparseCore 0:
  9.7 52.3 all-gather.1
where the time goes:
time: 554 us; the launch traced here: 553 us
  blocking collectives  183 us (33%)
  local copies, waits for them, and re-layouts  177 us (32%)
  starting transfers between devices  113 us (20%)
  waiting for transfers between devices  39.1 us (7%)
  other arithmetic  24.3 us (4%)
  between operations  16 us (3%)
    psum x1, blocking collectives, local(): traces = lax.psum(jnp.stack(recorded, axis=-1), ('gx', 'gy'))  183 us
    div x8, local copies, waits for them, and re-layouts, advance(): (2.0 * middle - (1.0 - damp) * previous + coef * laplace(extended) + inje...  134 us
    ppermute x16, starting transfers between devices, extended_2(): lax.ppermute(tail, axis, [(i, (i + 1) % count) for i in range(ends)])  92.2 us
    all_gather x1, waiting for transfers between devices, local(): piece = lax.all_gather(model_tiles, ('shot', 'gx'), axis=0, tiled=True)  24.6 us
    gather x8, local copies, waits for them, and re-layouts, sample(): field[:, jnp.clip(local_x, 0, size_x - 1), jnp.clip(local_y, 0, size_y -...  23.6 us
    ppermute x16, starting transfers between devices, extended_2(): lax.ppermute(head, axis, [((i + 1) % count, i) for i in range(ends)])  20.7 us
    div x8, other arithmetic, advance(): (2.0 * middle - (1.0 - damp) * previous + coef * laplace(extended) + inje...  16.9 us
    slice x16, local copies, waits for them, and re-layouts, depth_ahead(): return jnp.concatenate([field[..., reach:], filler], axis=-1)  12.5 us
  transfers between devices with their start and end apart: 33, of which 17 were waited for; matrix products, arithmetic and copies ran while one was open for 29% of the time, Pallas kernels for 0%

commit v1 on v0

--- a/solution.py
+++ b/solution.py
@@ -135,7 +135,7 @@
         recorded.append(sample(fresh, receiver_cells, x_start, y_start))
         previous = current
         current = fresh
-    traces = lax.psum(jnp.stack(recorded, axis=-1), ("gx", "gy"))
+    traces = jnp.sum(lax.all_gather(jnp.stack(recorded, axis=-1), ("gx", "gy")), axis=0)
     return (current[None], previous[None], traces[None])
 
 

time: 554 us -> 469 us (0.85)
  blocking collectives: 183 us -> 97.4 us
    psum x1 -> x0, blocking collectives: 183 us -> none  [local(): traces = lax.psum(jnp.stack(recorded, axis=-1), ('gx', 'gy'))]
    all_gather x0 -> x1, blocking collectives: none -> 97.4 us  [local(): lax.all_gather(jnp.stack(recorded, axis=-1), ('gx', 'gy'))]
  transfers between devices with their start and end apart: 33 -> 33, of which waited for: 17 -> 17; matrix products, arithmetic and copies ran while one was open for 29% -> 34% of each run, Pallas kernels for 0% -> 0%
where the time goes in v1:
time: 469 us; the launch traced here: 468 us
  local copies, waits for them, and re-layouts  177 us (38%)
  starting transfers between devices  113 us (24%)
  blocking collectives  97.4 us (21%)
  waiting for transfers between devices  39.1 us (8%)
  other arithmetic  24.9 us (5%)
  between operations  16 us (3%)
    div x8, local copies, waits for them, and re-layouts, advance(): (2.0 * middle - (1.0 - damp) * previous + coef * laplace(extended) + inje...  134 us
    all_gather x1, blocking collectives, local(): lax.all_gather(jnp.stack(recorded, axis=-1), ('gx', 'gy'))  97.4 us
    ppermute x16, starting transfers between devices, extended_2(): lax.ppermute(tail, axis, [(i, (i + 1) % count) for i in range(ends)])  92.2 us
    all_gather x1, waiting for transfers between devices, local(): piece = lax.all_gather(model_tiles, ('shot', 'gx'), axis=0, tiled=True)  24.6 us
    gather x8, local copies, waits for them, and re-layouts, sample(): field[:, jnp.clip(local_x, 0, size_x - 1), jnp.clip(local_y, 0, size_y -...  23.6 us
    ppermute x16, starting transfers between devices, extended_2(): lax.ppermute(head, axis, [((i + 1) % count, i) for i in range(ends)])  20.7 us
    div x8, other arithmetic, advance(): (2.0 * middle - (1.0 - damp) * previous + coef * laplace(extended) + inje...  16.9 us
    slice x16, local copies, waits for them, and re-layouts, depth_ahead(): return jnp.concatenate([field[..., reach:], filler], axis=-1)  12.5 us
  transfers between devices with their start and end apart: 33, of which 17 were waited for; matrix products, arithmetic and copies ran while one was open for 34% of the time, Pallas kernels for 0%

profile of v1, /device:TPU:0, one launch (start us, length us, event | category | flops | bytes accessed | tf_op | source)
XLA Modules:
  0.0 467.5 jit_solution(7927539147912254033)
XLA Ops:
  28.2 6.1 %collective-permute-start.3 = (f32[2,20,2,128]{3,2,1,0:T(2,128)S(1)}, f32[2,20,2,128]{3,2,1,0:T(2,128)S(1)}, u32[]{:S(2)}, u32[]{:S(2)}) collective-permute-start(f32[2,20,2,128]{3,2,1,0:T(2,128)S(1)} %get-tuple-element.57), channel_id=1, source_target_pairs={{0,1},{1,2},{2,3},{3,4},{4,5},{5,6},{6,7},{8,9},{9,10},{10,11},{11... | collective-permute-start | bytes 122888 | tf_op jit(solution)/shard_map/ppermute | solution.py:21
  37.5 24.6 %all-gather.3.cloned.1.call-done = f32[256,32,128]{2,1,0:T(8,128)} async-done(((f32[16,32,128]{2,1,0:T(8,128)}), f32[256,32,128]{2,1,0:T(8,128)}) %all-gather.3.cloned.1.call-update) | async-done | bytes 4194320 | tf_op jit(solution)/shard_map/all_gather | solution.py:113
  77.4 6.1 %collective-permute-start.7 = (f32[2,20,2,128]{3,2,1,0:T(2,128)S(1)}, f32[2,20,2,128]{3,2,1,0:T(2,128)S(1)}, u32[]{:S(2)}, u32[]{:S(2)}) collective-permute-start(f32[2,20,2,128]{3,2,1,0:T(2,128)S(1)} %get-tuple-element.53), channel_id=1, source_target_pairs={{0,1},{1,2},{2,3},{3,4},{4,5},{5,6},{6,7},{8,9},{9,10},{10,11},{11... | collective-permute-start | bytes 122888 | tf_op jit(solution)/shard_map/ppermute | solution.py:21
  84.4 16.7 %copy.514 = f32[2,16,32,128]{0,3,2,1:T(8,128)} copy(f32[2,16,32,128]{3,2,1,0:T(8,128)S(1)} %fusion.94) | data formatting | bytes 1048576 | tf_op jit(solution)/shard_map/div | solution.py:86
  107.5 5.0 %collective-permute-start.9 = (f32[2,2,32,128]{3,2,1,0:T(8,128)S(1)}, f32[2,2,32,128]{3,2,1,0:T(8,128)S(1)}, u32[]{:S(2)}, u32[]{:S(2)}) collective-permute-start(f32[2,2,32,128]{3,2,1,0:T(8,128)S(1)} %get-tuple-element.93), channel_id=1, source_target_pairs={{0,8},{8,16},{16,24},{1,9},{9,17},{17,25},{2,10},{10,18},{18,26},{... | collective-permute-start | bytes 196616 | tf_op jit(solution)/shard_map/ppermute | solution.py:21
  115.8 6.5 %collective-permute-start.11 = (f32[2,20,2,128]{3,2,1,0:T(2,128)S(1)}, f32[2,20,2,128]{3,2,1,0:T(2,128)S(1)}, u32[]{:S(2)}, u32[]{:S(2)}) collective-permute-start(f32[2,20,2,128]{3,2,1,0:T(2,128)S(1)} %get-tuple-element.49), channel_id=1, source_target_pairs={{0,1},{1,2},{2,3},{3,4},{4,5},{5,6},{6,7},{8,9},{9,10},{10,11},{11... | collective-permute-start | bytes 122888 | tf_op jit(solution)/shard_map/ppermute | solution.py:21
  123.2 16.7 %copy.515 = f32[2,16,32,128]{0,3,2,1:T(8,128)} copy(f32[2,16,32,128]{3,2,1,0:T(8,128)S(1)} %fusion.82) | data formatting | bytes 1048576 | tf_op jit(solution)/shard_map/div | solution.py:86
  146.4 4.9 %collective-permute-start.13 = (f32[2,2,32,128]{3,2,1,0:T(8,128)S(1)}, f32[2,2,32,128]{3,2,1,0:T(8,128)S(1)}, u32[]{:S(2)}, u32[]{:S(2)}) collective-permute-start(f32[2,2,32,128]{3,2,1,0:T(8,128)S(1)} %get-tuple-element.87), channel_id=1, source_target_pairs={{0,8},{8,16},{16,24},{1,9},{9,17},{17,25},{2,10},{10,18},{18,26},{... | collective-permute-start | bytes 196616 | tf_op jit(solution)/shard_map/ppermute | solution.py:21
  154.5 6.9 %collective-permute-start.15 = (f32[2,20,2,128]{3,2,1,0:T(2,128)S(1)}, f32[2,20,2,128]{3,2,1,0:T(2,128)S(1)}, u32[]{:S(2)}, u32[]{:S(2)}) collective-permute-start(f32[2,20,2,128]{3,2,1,0:T(2,128)S(1)} %get-tuple-element.45), channel_id=1, source_target_pairs={{0,1},{1,2},{2,3},{3,4},{4,5},{5,6},{6,7},{8,9},{9,10},{10,11},{11... | collective-permute-start | bytes 122888 | tf_op jit(solution)/shard_map/ppermute | solution.py:21
  162.4 16.7 %copy.516 = f32[2,16,32,128]{0,3,2,1:T(8,128)} copy(f32[2,16,32,128]{3,2,1,0:T(8,128)S(1)} %fusion.70) | data formatting | bytes 1048576 | tf_op jit(solution)/shard_map/div | solution.py:86
  185.6 4.9 %collective-permute-start.17 = (f32[2,2,32,128]{3,2,1,0:T(8,128)S(1)}, f32[2,2,32,128]{3,2,1,0:T(8,128)S(1)}, u32[]{:S(2)}, u32[]{:S(2)}) collective-permute-start(f32[2,2,32,128]{3,2,1,0:T(8,128)S(1)} %get-tuple-element.81), channel_id=1, source_target_pairs={{0,8},{8,16},{16,24},{1,9},{9,17},{17,25},{2,10},{10,18},{18,26},{... | collective-permute-start | bytes 196616 | tf_op jit(solution)/shard_map/ppermute | solution.py:21
  193.7 7.1 %collective-permute-start.19 = (f32[2,20,2,128]{3,2,1,0:T(2,128)S(1)}, f32[2,20,2,128]{3,2,1,0:T(2,128)S(1)}, u32[]{:S(2)}, u32[]{:S(2)}) collective-permute-start(f32[2,20,2,128]{3,2,1,0:T(2,128)S(1)} %get-tuple-element.41), channel_id=1, source_target_pairs={{0,1},{1,2},{2,3},{3,4},{4,5},{5,6},{6,7},{8,9},{9,10},{10,11},{11... | collective-permute-start | bytes 122888 | tf_op jit(solution)/shard_map/ppermute | solution.py:21
  201.7 16.7 %copy.517 = f32[2,16,32,128]{0,3,2,1:T(8,128)} copy(f32[2,16,32,128]{3,2,1,0:T(8,128)S(1)} %fusion.58) | data formatting | bytes 1048576 | tf_op jit(solution)/shard_map/div | solution.py:86
  224.9 4.9 %collective-permute-start.21 = (f32[2,2,32,128]{3,2,1,0:T(8,128)S(1)}, f32[2,2,32,128]{3,2,1,0:T(8,128)S(1)}, u32[]{:S(2)}, u32[]{:S(2)}) collective-permute-start(f32[2,2,32,128]{3,2,1,0:T(8,128)S(1)} %get-tuple-element.75), channel_id=1, source_target_pairs={{0,8},{8,16},{16,24},{1,9},{9,17},{17,25},{2,10},{10,18},{18,26},{... | collective-permute-start | bytes 196616 | tf_op jit(solution)/shard_map/ppermute | solution.py:21
  233.0 6.9 %collective-permute-start.23 = (f32[2,20,2,128]{3,2,1,0:T(2,128)S(1)}, f32[2,20,2,128]{3,2,1,0:T(2,128)S(1)}, u32[]{:S(2)}, u32[]{:S(2)}) collective-permute-start(f32[2,20,2,128]{3,2,1,0:T(2,128)S(1)} %get-tuple-element.37), channel_id=1, source_target_pairs={{0,1},{1,2},{2,3},{3,4},{4,5},{5,6},{6,7},{8,9},{9,10},{10,11},{11... | collective-permute-start | bytes 122888 | tf_op jit(solution)/shard_map/ppermute | solution.py:21
  240.9 16.7 %copy.518 = f32[2,16,32,128]{0,3,2,1:T(8,128)} copy(f32[2,16,32,128]{3,2,1,0:T(8,128)S(1)} %fusion.46) | data formatting | bytes 1048576 | tf_op jit(solution)/shard_map/div | solution.py:86
  264.1 4.9 %collective-permute-start.25 = (f32[2,2,32,128]{3,2,1,0:T(8,128)S(1)}, f32[2,2,32,128]{3,2,1,0:T(8,128)S(1)}, u32[]{:S(2)}, u32[]{:S(2)}) collective-permute-start(f32[2,2,32,128]{3,2,1,0:T(8,128)S(1)} %get-tuple-element.69), channel_id=1, source_target_pairs={{0,8},{8,16},{16,24},{1,9},{9,17},{17,25},{2,10},{10,18},{18,26},{... | collective-permute-start | bytes 196616 | tf_op jit(solution)/shard_map/ppermute | solution.py:21
  272.2 6.9 %collective-permute-start.27 = (f32[2,20,2,128]{3,2,1,0:T(2,128)S(1)}, f32[2,20,2,128]{3,2,1,0:T(2,128)S(1)}, u32[]{:S(2)}, u32[]{:S(2)}) collective-permute-start(f32[2,20,2,128]{3,2,1,0:T(2,128)S(1)} %get-tuple-element.33), channel_id=1, source_target_pairs={{0,1},{1,2},{2,3},{3,4},{4,5},{5,6},{6,7},{8,9},{9,10},{10,11},{11... | collective-permute-start | bytes 122888 | tf_op jit(solution)/shard_map/ppermute | solution.py:21
  280.1 16.7 %copy.519 = f32[2,16,32,128]{0,3,2,1:T(8,128)} copy(f32[2,16,32,128]{3,2,1,0:T(8,128)S(1)} %fusion.34) | data formatting | bytes 1048576 | tf_op jit(solution)/shard_map/div | solution.py:86
  303.2 4.9 %collective-permute-start.29 = (f32[2,2,32,128]{3,2,1,0:T(8,128)S(1)}, f32[2,2,32,128]{3,2,1,0:T(8,128)S(1)}, u32[]{:S(2)}, u32[]{:S(2)}) collective-permute-start(f32[2,2,32,128]{3,2,1,0:T(8,128)S(1)} %get-tuple-element.63), channel_id=1, source_target_pairs={{0,8},{8,16},{16,24},{1,9},{9,17},{17,25},{2,10},{10,18},{18,26},{... | collective-permute-start | bytes 196616 | tf_op jit(solution)/shard_map/ppermute | solution.py:21
  311.3 7.2 %collective-permute-start.31 = (f32[2,20,2,128]{3,2,1,0:T(2,128)S(1)}, f32[2,20,2,128]{3,2,1,0:T(2,128)S(1)}, u32[]{:S(2)}, u32[]{:S(2)}) collective-permute-start(f32[2,20,2,128]{3,2,1,0:T(2,128)S(1)} %get-tuple-element.29), channel_id=1, source_target_pairs={{0,1},{1,2},{2,3},{3,4},{4,5},{5,6},{6,7},{8,9},{9,10},{10,11},{11... | collective-permute-start | bytes 122888 | tf_op jit(solution)/shard_map/ppermute | solution.py:21
  319.5 16.7 %copy.520 = f32[2,16,32,128]{0,3,2,1:T(8,128)} copy(f32[2,16,32,128]{3,2,1,0:T(8,128)S(1)} %fusion.22) | data formatting | bytes 1048576 | tf_op jit(solution)/shard_map/div | solution.py:86
  341.3 16.8 %copy.521 = f32[2,16,32,128]{0,3,2,1:T(8,128)} copy(f32[2,16,32,128]{3,2,1,0:T(8,128)S(1)} %fusion.10) | data formatting | bytes 1048576 | tf_op jit(solution)/shard_map/div | solution.py:86
  362.6 97.4 %all-gather = f32[64,256,8]{1,2,0:T(8,128)S(1)} all-gather(f32[2,256,8]{1,2,0:T(8,128)S(1)} %stack.2), channel_id=2, replica_groups=mesh['shot'=4,'gx'=4,'gy'=8] {'gx','gy'}, dimensions={0}, use_global_device_ids=true | all-gather | bytes 540672 | tf_op jit(solution)/shard_map/all_gather | solution.py:138
  (165 shorter events, 112.8 us)
Async XLA Ops:
  7.2 54.9 %all-gather.3.cloned.1.call-start = ((), (), s32[]{:S(2)}) async-start(), calls=%async_computation | async-start | bytes 4456448 | tf_op jit(solution)/shard_map/all_gather | solution.py:113
  8.8 17.0 %collective-permute-start = (f32[2,2,32,128]{3,2,1,0:T(8,128)S(1)}, f32[2,2,32,128]{3,2,1,0:T(8,128)S(1)}, u32[]{:S(2)}, u32[]{:S(2)}) collective-permute-start(f32[2,2,32,128]{3,2,1,0:T(8,128)S(1)} %get-tuple-element.104), channel_id=1, source_target_pairs={{8,0},{16,8},{24,16},{9,1},{17,9},{25,17},{10,2},{18,10},{26,18},{... | collective-permute-start | bytes 196616 | tf_op jit(solution)/shard_map/ppermute | solution.py:23
  10.1 15.8 %collective-permute-start.1 = (f32[2,2,32,128]{3,2,1,0:T(8,128)S(1)}, f32[2,2,32,128]{3,2,1,0:T(8,128)S(1)}, u32[]{:S(2)}, u32[]{:S(2)}) collective-permute-start(f32[2,2,32,128]{3,2,1,0:T(8,128)S(1)} %get-tuple-element.105), channel_id=1, source_target_pairs={{0,8},{8,16},{16,24},{1,9},{9,17},{17,25},{2,10},{10,18},{18,26},{... | collective-permute-start | bytes 196616 | tf_op jit(solution)/shard_map/ppermute | solution.py:21
  26.9 7.7 %collective-permute-start.2 = (f32[2,20,2,128]{3,2,1,0:T(2,128)S(1)}, f32[2,20,2,128]{3,2,1,0:T(2,128)S(1)}, u32[]{:S(2)}, u32[]{:S(2)}) collective-permute-start(f32[2,20,2,128]{3,2,1,0:T(2,128)S(1)} %get-tuple-element.56), channel_id=1, source_target_pairs={{1,0},{2,1},{3,2},{4,3},{5,4},{6,5},{7,6},{9,8},{10,9},{11,10},{12... | collective-permute-start | bytes 122888 | tf_op jit(solution)/shard_map/ppermute | solution.py:23
  28.2 7.9 %collective-permute-start.3 = (f32[2,20,2,128]{3,2,1,0:T(2,128)S(1)}, f32[2,20,2,128]{3,2,1,0:T(2,128)S(1)}, u32[]{:S(2)}, u32[]{:S(2)}) collective-permute-start(f32[2,20,2,128]{3,2,1,0:T(2,128)S(1)} %get-tuple-element.57), channel_id=1, source_target_pairs={{0,1},{1,2},{2,3},{3,4},{4,5},{5,6},{6,7},{8,9},{9,10},{10,11},{11... | collective-permute-start | bytes 122888 | tf_op jit(solution)/shard_map/ppermute | solution.py:21
  68.1 6.8 %collective-permute-start.4 = (f32[2,2,32,128]{3,2,1,0:T(8,128)S(1)}, f32[2,2,32,128]{3,2,1,0:T(8,128)S(1)}, u32[]{:S(2)}, u32[]{:S(2)}) collective-permute-start(f32[2,2,32,128]{3,2,1,0:T(8,128)S(1)} %get-tuple-element.98), channel_id=1, source_target_pairs={{8,0},{16,8},{24,16},{9,1},{17,9},{25,17},{10,2},{18,10},{26,18},{... | collective-permute-start | bytes 196616 | tf_op jit(solution)/shard_map/ppermute | solution.py:23
  76.1 28.0 %collective-permute-start.6 = (f32[2,20,2,128]{3,2,1,0:T(2,128)S(1)}, f32[2,20,2,128]{3,2,1,0:T(2,128)S(1)}, u32[]{:S(2)}, u32[]{:S(2)}) collective-permute-start(f32[2,20,2,128]{3,2,1,0:T(2,128)S(1)} %get-tuple-element.52), channel_id=1, source_target_pairs={{1,0},{2,1},{3,2},{4,3},{5,4},{6,5},{7,6},{9,8},{10,9},{11,10},{12... | collective-permute-start | bytes 122888 | tf_op jit(solution)/shard_map/ppermute | solution.py:23
  77.4 26.7 %collective-permute-start.7 = (f32[2,20,2,128]{3,2,1,0:T(2,128)S(1)}, f32[2,20,2,128]{3,2,1,0:T(2,128)S(1)}, u32[]{:S(2)}, u32[]{:S(2)}) collective-permute-start(f32[2,20,2,128]{3,2,1,0:T(2,128)S(1)} %get-tuple-element.53), channel_id=1, source_target_pairs={{0,1},{1,2},{2,3},{3,4},{4,5},{5,6},{6,7},{8,9},{9,10},{10,11},{11... | collective-permute-start | bytes 122888 | tf_op jit(solution)/shard_map/ppermute | solution.py:21
  107.5 6.9 %collective-permute-start.9 = (f32[2,2,32,128]{3,2,1,0:T(8,128)S(1)}, f32[2,2,32,128]{3,2,1,0:T(8,128)S(1)}, u32[]{:S(2)}, u32[]{:S(2)}) collective-permute-start(f32[2,2,32,128]{3,2,1,0:T(8,128)S(1)} %get-tuple-element.93), channel_id=1, source_target_pairs={{0,8},{8,16},{16,24},{1,9},{9,17},{17,25},{2,10},{10,18},{18,26},{... | collective-permute-start | bytes 196616 | tf_op jit(solution)/shard_map/ppermute | solution.py:21
  114.5 28.5 %collective-permute-start.10 = (f32[2,20,2,128]{3,2,1,0:T(2,128)S(1)}, f32[2,20,2,128]{3,2,1,0:T(2,128)S(1)}, u32[]{:S(2)}, u32[]{:S(2)}) collective-permute-start(f32[2,20,2,128]{3,2,1,0:T(2,128)S(1)} %get-tuple-element.48), channel_id=1, source_target_pairs={{1,0},{2,1},{3,2},{4,3},{5,4},{6,5},{7,6},{9,8},{10,9},{11,10},{12... | collective-permute-start | bytes 122888 | tf_op jit(solution)/shard_map/ppermute | solution.py:23
  115.8 27.2 %collective-permute-start.11 = (f32[2,20,2,128]{3,2,1,0:T(2,128)S(1)}, f32[2,20,2,128]{3,2,1,0:T(2,128)S(1)}, u32[]{:S(2)}, u32[]{:S(2)}) collective-permute-start(f32[2,20,2,128]{3,2,1,0:T(2,128)S(1)} %get-tuple-element.49), channel_id=1, source_target_pairs={{0,1},{1,2},{2,3},{3,4},{4,5},{5,6},{6,7},{8,9},{9,10},{10,11},{11... | collective-permute-start | bytes 122888 | tf_op jit(solution)/shard_map/ppermute | solution.py:21
  146.4 6.8 %collective-permute-start.13 = (f32[2,2,32,128]{3,2,1,0:T(8,128)S(1)}, f32[2,2,32,128]{3,2,1,0:T(8,128)S(1)}, u32[]{:S(2)}, u32[]{:S(2)}) collective-permute-start(f32[2,2,32,128]{3,2,1,0:T(8,128)S(1)} %get-tuple-element.87), channel_id=1, source_target_pairs={{0,8},{8,16},{16,24},{1,9},{9,17},{17,25},{2,10},{10,18},{18,26},{... | collective-permute-start | bytes 196616 | tf_op jit(solution)/shard_map/ppermute | solution.py:21
  153.2 28.9 %collective-permute-start.14 = (f32[2,20,2,128]{3,2,1,0:T(2,128)S(1)}, f32[2,20,2,128]{3,2,1,0:T(2,128)S(1)}, u32[]{:S(2)}, u32[]{:S(2)}) collective-permute-start(f32[2,20,2,128]{3,2,1,0:T(2,128)S(1)} %get-tuple-element.44), channel_id=1, source_target_pairs={{1,0},{2,1},{3,2},{4,3},{5,4},{6,5},{7,6},{9,8},{10,9},{11,10},{12... | collective-permute-start | bytes 122888 | tf_op jit(solution)/shard_map/ppermute | solution.py:23
  154.5 27.6 %collective-permute-start.15 = (f32[2,20,2,128]{3,2,1,0:T(2,128)S(1)}, f32[2,20,2,128]{3,2,1,0:T(2,128)S(1)}, u32[]{:S(2)}, u32[]{:S(2)}) collective-permute-start(f32[2,20,2,128]{3,2,1,0:T(2,128)S(1)} %get-tuple-element.45), channel_id=1, source_target_pairs={{0,1},{1,2},{2,3},{3,4},{4,5},{5,6},{6,7},{8,9},{9,10},{10,11},{11... | collective-permute-start | bytes 122888 | tf_op jit(solution)/shard_map/ppermute | solution.py:21
  185.6 6.8 %collective-permute-start.17 = (f32[2,2,32,128]{3,2,1,0:T(8,128)S(1)}, f32[2,2,32,128]{3,2,1,0:T(8,128)S(1)}, u32[]{:S(2)}, u32[]{:S(2)}) collective-permute-start(f32[2,2,32,128]{3,2,1,0:T(8,128)S(1)} %get-tuple-element.81), channel_id=1, source_target_pairs={{0,8},{8,16},{16,24},{1,9},{9,17},{17,25},{2,10},{10,18},{18,26},{... | collective-permute-start | bytes 196616 | tf_op jit(solution)/shard_map/ppermute | solution.py:21
  192.4 29.1 %collective-permute-start.18 = (f32[2,20,2,128]{3,2,1,0:T(2,128)S(1)}, f32[2,20,2,128]{3,2,1,0:T(2,128)S(1)}, u32[]{:S(2)}, u32[]{:S(2)}) collective-permute-start(f32[2,20,2,128]{3,2,1,0:T(2,128)S(1)} %get-tuple-element.40), channel_id=1, source_target_pairs={{1,0},{2,1},{3,2},{4,3},{5,4},{6,5},{7,6},{9,8},{10,9},{11,10},{12... | collective-permute-start | bytes 122888 | tf_op jit(solution)/shard_map/ppermute | solution.py:23
  193.7 27.8 %collective-permute-start.19 = (f32[2,20,2,128]{3,2,1,0:T(2,128)S(1)}, f32[2,20,2,128]{3,2,1,0:T(2,128)S(1)}, u32[]{:S(2)}, u32[]{:S(2)}) collective-permute-start(f32[2,20,2,128]{3,2,1,0:T(2,128)S(1)} %get-tuple-element.41), channel_id=1, source_target_pairs={{0,1},{1,2},{2,3},{3,4},{4,5},{5,6},{6,7},{8,9},{9,10},{10,11},{11... | collective-permute-start | bytes 122888 | tf_op jit(solution)/shard_map/ppermute | solution.py:21
  231.7 28.9 %collective-permute-start.22 = (f32[2,20,2,128]{3,2,1,0:T(2,128)S(1)}, f32[2,20,2,128]{3,2,1,0:T(2,128)S(1)}, u32[]{:S(2)}, u32[]{:S(2)}) collective-permute-start(f32[2,20,2,128]{3,2,1,0:T(2,128)S(1)} %get-tuple-element.36), channel_id=1, source_target_pairs={{1,0},{2,1},{3,2},{4,3},{5,4},{6,5},{7,6},{9,8},{10,9},{11,10},{12... | collective-permute-start | bytes 122888 | tf_op jit(solution)/shard_map/ppermute | solution.py:23
  233.0 27.6 %collective-permute-start.23 = (f32[2,20,2,128]{3,2,1,0:T(2,128)S(1)}, f32[2,20,2,128]{3,2,1,0:T(2,128)S(1)}, u32[]{:S(2)}, u32[]{:S(2)}) collective-permute-start(f32[2,20,2,128]{3,2,1,0:T(2,128)S(1)} %get-tuple-element.37), channel_id=1, source_target_pairs={{0,1},{1,2},{2,3},{3,4},{4,5},{5,6},{6,7},{8,9},{9,10},{10,11},{11... | collective-permute-start | bytes 122888 | tf_op jit(solution)/shard_map/ppermute | solution.py:21
  264.1 6.8 %collective-permute-start.25 = (f32[2,2,32,128]{3,2,1,0:T(8,128)S(1)}, f32[2,2,32,128]{3,2,1,0:T(8,128)S(1)}, u32[]{:S(2)}, u32[]{:S(2)}) collective-permute-start(f32[2,2,32,128]{3,2,1,0:T(8,128)S(1)} %get-tuple-element.69), channel_id=1, source_target_pairs={{0,8},{8,16},{16,24},{1,9},{9,17},{17,25},{2,10},{10,18},{18,26},{... | collective-permute-start | bytes 196616 | tf_op jit(solution)/shard_map/ppermute | solution.py:21
  270.9 28.9 %collective-permute-start.26 = (f32[2,20,2,128]{3,2,1,0:T(2,128)S(1)}, f32[2,20,2,128]{3,2,1,0:T(2,128)S(1)}, u32[]{:S(2)}, u32[]{:S(2)}) collective-permute-start(f32[2,20,2,128]{3,2,1,0:T(2,128)S(1)} %get-tuple-element.32), channel_id=1, source_target_pairs={{1,0},{2,1},{3,2},{4,3},{5,4},{6,5},{7,6},{9,8},{10,9},{11,10},{12... | collective-permute-start | bytes 122888 | tf_op jit(solution)/shard_map/ppermute | solution.py:23
  272.2 27.6 %collective-permute-start.27 = (f32[2,20,2,128]{3,2,1,0:T(2,128)S(1)}, f32[2,20,2,128]{3,2,1,0:T(2,128)S(1)}, u32[]{:S(2)}, u32[]{:S(2)}) collective-permute-start(f32[2,20,2,128]{3,2,1,0:T(2,128)S(1)} %get-tuple-element.33), channel_id=1, source_target_pairs={{0,1},{1,2},{2,3},{3,4},{4,5},{5,6},{6,7},{8,9},{9,10},{10,11},{11... | collective-permute-start | bytes 122888 | tf_op jit(solution)/shard_map/ppermute | solution.py:21
  310.0 29.1 %collective-permute-start.30 = (f32[2,20,2,128]{3,2,1,0:T(2,128)S(1)}, f32[2,20,2,128]{3,2,1,0:T(2,128)S(1)}, u32[]{:S(2)}, u32[]{:S(2)}) collective-permute-start(f32[2,20,2,128]{3,2,1,0:T(2,128)S(1)} %get-tuple-element.28), channel_id=1, source_target_pairs={{1,0},{2,1},{3,2},{4,3},{5,4},{6,5},{7,6},{9,8},{10,9},{11,10},{12... | collective-permute-start | bytes 122888 | tf_op jit(solution)/shard_map/ppermute | solution.py:23
  311.3 27.8 %collective-permute-start.31 = (f32[2,20,2,128]{3,2,1,0:T(2,128)S(1)}, f32[2,20,2,128]{3,2,1,0:T(2,128)S(1)}, u32[]{:S(2)}, u32[]{:S(2)}) collective-permute-start(f32[2,20,2,128]{3,2,1,0:T(2,128)S(1)} %get-tuple-element.29), channel_id=1, source_target_pairs={{0,1},{1,2},{2,3},{3,4},{4,5},{5,6},{6,7},{8,9},{9,10},{10,11},{11... | collective-permute-start | bytes 122888 | tf_op jit(solution)/shard_map/ppermute | solution.py:21
  (22 other events, 631.6 us)
Sparse Core Ops, SparseCore 0:
  9.7 52.3 all-gather.2
